TPU v7x, 32 devices: a whole 2x2x4 slice. The times are simulated.
32 devices in a mesh: gx: 4 (over z), gy: 4 (over x, core), gz: 2 (over y).
Axes of the slice: x: 2, y: 2, z: 4, core: 2. Of those that a mesh axis runs over, the one named last changes fastest.
Arguments:
- response: float32 [32, 32, 12, 128], P('gx', 'gy', 'gz'), may hold values from -3 to 3
- source: float32 [32, 32, 12, 128], P('gx', 'gy', 'gz'), may hold values from -6 to 6
- occupied: float32 [32, 32, 12, 2048], P('gx', 'gy', 'gz'), may hold values from -0.0546875 to 0.0546875
- potential: float32 [32, 32, 12], P('gx', 'gy', 'gz'), may hold values from 0 to 2
- energy_shift: float32 [128], replicated, may hold values from 0.5 to 2
Outputs:
- updated: float32 [32, 32, 12, 128], P('gx', 'gy', 'gz')
- projected: float32 [32, 32, 12, 128], P('gx', 'gy', 'gz')
All inputs are finite; a program needn't handle non-finite values.
Results may differ from a plain program's by a relative error of at most 0.00011.
Values sent between devices are 32-bit elements; how exact they have to be, the bound alone decides.
No kernel may reach another device: no remote copies, remote signals or barrier semaphores. Data moves between devices by JAX's collectives and lax.ppermute only.
A program may use at most 64 MiB of HBM per device.

v0:
```python
import jax
import jax.numpy as jnp
from jax import lax
from jax.sharding import PartitionSpec as P

stencil_weights = (
    -5369.0 / 1800.0,
    12.0 / 7.0,
    -15.0 / 56.0,
    10.0 / 189.0,
    -1.0 / 112.0,
    2.0 / 1925.0,
    -1.0 / 16632.0,
)
damping = 0.1
margin = 6


def with_halo(block, sides, width):
    for axis, dim in sides:
        count = lax.axis_size(axis)
        forward = [(i, i + 1) for i in range(count - 1)]
        backward = [(target, source) for source, target in forward]
        low = lax.ppermute(
            lax.slice_in_dim(block, block.shape[dim] - width, None, axis=dim), axis, forward
        )
        high = lax.ppermute(lax.slice_in_dim(block, 0, width, axis=dim), axis, backward)
        block = jnp.concatenate([low, block, high], axis=dim)
    return block


def laplacian(padded, span_first, span_second, span_third):
    centre = padded[
        margin : margin + span_first, margin : margin + span_second, margin : margin + span_third
    ]
    summed = 3.0 * stencil_weights[0] * centre
    for offset in range(1, margin + 1):
        beside = padded[
            margin + offset : margin + offset + span_first,
            margin : margin + span_second,
            margin : margin + span_third,
        ]
        beside = (
            beside
            + padded[
                margin - offset : margin - offset + span_first,
                margin : margin + span_second,
                margin : margin + span_third,
            ]
        )
        beside = (
            beside
            + padded[
                margin : margin + span_first,
                margin + offset : margin + offset + span_second,
                margin : margin + span_third,
            ]
        )
        beside = (
            beside
            + padded[
                margin : margin + span_first,
                margin - offset : margin - offset + span_second,
                margin : margin + span_third,
            ]
        )
        beside = (
            beside
            + padded[
                margin : margin + span_first,
                margin : margin + span_second,
                margin + offset : margin + offset + span_third,
            ]
        )
        beside = (
            beside
            + padded[
                margin : margin + span_first,
                margin : margin + span_second,
                margin - offset : margin - offset + span_third,
            ]
        )
        summed = summed + stencil_weights[offset] * beside
    return (centre, summed)


def residual_of(padded, potential, energy_shift, source):
    span_first, span_second, span_third = potential.shape
    centre, summed = laplacian(padded, span_first, span_second, span_third)
    return -0.5 * summed + (potential[:, :, :, None] + energy_shift) * centre + source


def shards(response, source, occupied, potential, energy_shift):
    span_first, span_second, span_third, orbitals = response.shape
    cell_count = span_first * span_second * span_third
    flat_occ = occupied.reshape(cell_count, occupied.shape[3])
    updated = response
    padded = with_halo(updated, (("gx", 0), ("gy", 1), ("gz", 2)), 6)
    residual = residual_of(padded, potential, energy_shift, source)
    flat_res = residual.reshape(cell_count, orbitals)
    partial_intersection = lax.dot_general(
        flat_occ,
        flat_res,
        (((0,), (0,)), ((), ())),
        precision=lax.Precision.HIGHEST,
        preferred_element_type=jnp.float32,
    )
    share = lax.psum_scatter(partial_intersection, ("gy", "gz"), scatter_dimension=0, tiled=True)
    share = lax.psum(share, "gx")
    removed = jnp.dot(
        flat_occ,
        lax.all_gather(share, ("gy", "gz"), axis=0, tiled=True),
        precision=lax.Precision.HIGHEST,
        preferred_element_type=jnp.float32,
    )
    projected = (flat_res - removed).reshape(updated.shape)
    updated = updated - damping * projected
    return (updated, projected)


def solution(mesh):
    return jax.shard_map(
        shards,
        mesh=mesh,
        in_specs=(
            P("gx", "gy", "gz", None),
            P("gx", "gy", "gz", None),
            P("gx", "gy", "gz", None),
            P("gx", "gy", "gz"),
            P(),
        ),
        out_specs=(P("gx", "gy", "gz", None), P("gx", "gy", "gz", None)),
        check_vma=False,
    )
```

profile of v0, /device:TPU:0, one launch (start us, length us, event | category | flops | bytes accessed | tf_op | source)
XLA Modules:
  0.0 182.8 jit_solution(17553583483827970159)
XLA Ops:
  7.2 0.0 reduce-scatter.2.cloned.1.call-start
  7.2 1.0 fusion.49
  8.2 5.0 %collective-permute-start.1 = (f32[6,8,6,128]{3,1,2,0:T(8,128)S(1)}, f32[6,8,6,128]{3,1,2,0:T(8,128)S(1)}, u32[]{:S(2)}, u32[]{:S(2)}) collective-permute-start(f32[6,8,6,128]{3,1,2,0:T(8,128)S(1)} %get-tuple-element.12), channel_id=1, source_target_pairs={{0,8},{8,16},{16,24},{1,9},{9,17},{17,25},{2,10},{10,18},{18,26},{... | collective-permute-start | bytes 442376 | tf_op jit(solution)/shard_map/ppermute | solution.py:24
  13.2 1.3 collective-permute-start
  14.5 1.8 collective-permute-done.1
  16.3 1.0 constant_dynamic-update-slice_fusion.1
  17.3 3.1 %collective-permute-done = f32[6,8,6,128]{3,1,2,0:T(8,128)S(1)} collective-permute-done((f32[6,8,6,128]{3,1,2,0:T(8,128)S(1)}, f32[6,8,6,128]{3,1,2,0:T(8,128)S(1)}, u32[]{:S(2)}, u32[]{:S(2)}) %collective-permute-start) | collective-permute-done | bytes 147488 | tf_op jit(solution)/shard_map/ppermute | solution.py:27
  20.4 0.1 fusion.48
  20.5 1.3 collective-permute-start.2
  21.8 0.0 copy-start.3
  21.8 0.0 copy-start.1
  21.8 0.0 copy-start.2
  21.8 0.0 copy-start.4
  21.8 3.2 %collective-permute-start.3 = (f32[20,6,6,128]{3,1,2,0:T(8,128)S(1)}, f32[20,6,6,128]{3,1,2,0:T(8,128)S(1)}, u32[]{:S(2)}, u32[]{:S(2)}) collective-permute-start(f32[20,6,6,128]{3,1,2,0:T(8,128)S(1)} %get-tuple-element.7), channel_id=1, source_target_pairs={{0,2},{2,4},{4,6},{1,3},{3,5},{5,7},{8,10},{10,12},{12,14},{9,11},... | collective-permute-start | bytes 1105928 | tf_op jit(solution)/shard_map/ppermute | solution.py:24
  25.0 0.0 collective-permute-done.2
  25.1 1.4 collective-permute-done.3
  26.5 0.2 pad_maximum_fusion
  26.7 3.5 %collective-permute-start.5 = (f32[20,20,6,128]{3,1,2,0:T(8,128)S(1)}, f32[20,20,6,128]{3,1,2,0:T(8,128)S(1)}, u32[]{:S(2)}, u32[]{:S(2)}) collective-permute-start(f32[20,20,6,128]{3,1,2,0:T(8,128)S(1)} %pad_maximum_fusion), channel_id=1, source_target_pairs={{0,1},{2,3},{4,5},{6,7},{8,9},{10,11},{12,13},{14,15},{16,17},{18,... | collective-permute-start | bytes 3686408 | tf_op jit(solution)/shard_map/ppermute | solution.py:24
  30.2 1.3 collective-permute-start.4
  31.5 0.0 copy-done.3
  31.6 26.8 %collective-permute-done.5 = f32[20,20,6,128]{3,1,2,0:T(8,128)S(1)} collective-permute-done((f32[20,20,6,128]{3,1,2,0:T(8,128)S(1)}, f32[20,20,6,128]{3,1,2,0:T(8,128)S(1)}, u32[]{:S(2)}, u32[]{:S(2)}) %collective-permute-start.5) | collective-permute-done | bytes 1228832 | tf_op jit(solution)/shard_map/ppermute | solution.py:24
  58.4 4.8 %collective-permute-done.4 = f32[20,20,6,128]{3,1,2,0:T(8,128)S(1)} collective-permute-done((f32[20,20,6,128]{3,1,2,0:T(8,128)S(1)}, f32[20,20,6,128]{3,1,2,0:T(8,128)S(1)}, u32[]{:S(2)}, u32[]{:S(2)}) %collective-permute-start.4) | collective-permute-done | bytes 1228832 | tf_op jit(solution)/shard_map/ppermute | solution.py:27
  63.1 0.0 copy-done.1
  63.1 0.0 copy-done.2
  63.1 0.0 copy-done.4
  63.1 0.0 copy-start
  63.2 0.9 fusion.10
  64.1 1.0 copy-done
  65.0 3.0 %convolution_bitcast_fusion = f32[2048,128]{0,1:T(8,128)} fusion(f32[8,8,6,128]{3,1,2,0:T(8,128)S(1)} %fusion.10, f32[8,8,6,2048]{3,1,2,0:T(8,128)S(1)} %copy-done), kind=kOutput, calls=%fused_computation | convolution fusion | flops 1207959552 | bytes 4390912 | tf_op jit(solution)/shard_map/dot_general | solution.py:101
  68.1 0.0 reduce-scatter.2.cloned.1.call-update
  68.1 0.0 all-reduce.2.cloned.1.call-start
  68.1 38.7 %reduce-scatter.2.cloned.1.call-done = f32[256,128]{0,1:T(8,128)} async-done(((f32[2048,128]{0,1:T(8,128)}), f32[256,128]{0,1:T(8,128)}) %reduce-scatter.2.cloned.1.call-update) | async-done | bytes 131088 | tf_op jit(solution)/shard_map/reduce_scatter | solution.py:108
  106.8 0.0 all-reduce.2.cloned.1.call-update
  106.8 0.0 all-gather.2.cloned.1.call-start
  106.8 36.9 %all-reduce.2.cloned.1.call-done = f32[256,128]{0,1:T(8,128)} async-done(((f32[256,128]{0,1:T(8,128)}), f32[256,128]{0,1:T(8,128)}) %all-reduce.2.cloned.1.call-update) | async-done | bytes 131088 | tf_op jit(solution)/shard_map/psum | solution.py:109
  143.8 0.0 all-gather.2.cloned.1.call-update
  143.8 3.8 %copy.13 = f32[8,8,6,2048]{3,2,1,0:T(8,128)} copy(f32[8,8,6,2048]{3,1,2,0:T(8,128)S(1)} %copy-done) | data formatting | bytes 6291456 | tf_op args[2]
  147.6 3.1 %reshape.16 = f32[384,2048]{1,0:T(8,128)S(1)} reshape(f32[8,8,6,2048]{3,2,1,0:T(8,128)} %copy.13) | data formatting | bytes 6291456 | tf_op jit(solution)/shard_map/reshape | solution.py:96
  150.7 0.7 copy.12
  151.4 1.7 reshape.15
  153.1 1.1 copy.14
  154.1 14.8 %all-gather.2.cloned.1.call-done = f32[2048,128]{0,1:T(8,128)} async-done(((f32[256,128]{0,1:T(8,128)}), f32[2048,128]{0,1:T(8,128)}) %all-gather.2.cloned.1.call-update) | async-done | bytes 1048592 | tf_op jit(solution)/shard_map/all_gather | solution.py:112
  168.9 4.8 %fusion = f32[384,128]{0,1:T(8,128)} fusion(f32[384,128]{0,1:T(8,128)S(1)} %copy.14, f32[2048,128]{0,1:T(8,128)} %all-gather.2.cloned.1.call-done, f32[384,2048]{1,0:T(8,128)S(1)} %reshape.16), kind=kOutput, calls=%fused_computation.23 | convolution fusion | flops 1208008704 | bytes 4587520 | tf_op jit(solution)/shard_map/dot_general | solution.py:110
  173.7 1.1 copy.15
  174.8 0.7 copy.18
  175.5 0.1 copy_subtract_fusion
  175.6 0.7 copy.17
  (4 shorter events, 0.1 us)
Async XLA Ops:
  7.2 99.6 %reduce-scatter.2.cloned.1.call-start = ((), (), s32[]{:S(2)}) async-start(), calls=%async_computation.1 | async-start | bytes 1179648 | tf_op jit(solution)/shard_map/reduce_scatter | solution.py:108
  8.2 8.1 %collective-permute-start.1 = (f32[6,8,6,128]{3,1,2,0:T(8,128)S(1)}, f32[6,8,6,128]{3,1,2,0:T(8,128)S(1)}, u32[]{:S(2)}, u32[]{:S(2)}) collective-permute-start(f32[6,8,6,128]{3,1,2,0:T(8,128)S(1)} %get-tuple-element.12), channel_id=1, source_target_pairs={{0,8},{8,16},{16,24},{1,9},{9,17},{17,25},{2,10},{10,18},{18,26},{... | collective-permute-start | bytes 442376 | tf_op jit(solution)/shard_map/ppermute | solution.py:24
  13.2 7.2 %collective-permute-start = (f32[6,8,6,128]{3,1,2,0:T(8,128)S(1)}, f32[6,8,6,128]{3,1,2,0:T(8,128)S(1)}, u32[]{:S(2)}, u32[]{:S(2)}) collective-permute-start(f32[6,8,6,128]{3,1,2,0:T(8,128)S(1)} %get-tuple-element.11), channel_id=1, source_target_pairs={{8,0},{16,8},{24,16},{9,1},{17,9},{25,17},{10,2},{18,10},{26,18},{... | collective-permute-start | bytes 442376 | tf_op jit(solution)/shard_map/ppermute | solution.py:27
  20.5 4.6 %collective-permute-start.2 = (f32[20,6,6,128]{3,1,2,0:T(8,128)S(1)}, f32[20,6,6,128]{3,1,2,0:T(8,128)S(1)}, u32[]{:S(2)}, u32[]{:S(2)}) collective-permute-start(f32[20,6,6,128]{3,1,2,0:T(8,128)S(1)} %get-tuple-element.6), channel_id=1, source_target_pairs={{2,0},{4,2},{6,4},{3,1},{5,3},{7,5},{10,8},{12,10},{14,12},{11,9},... | collective-permute-start | bytes 1105928 | tf_op jit(solution)/shard_map/ppermute | solution.py:27
  21.8 9.7 %copy-start.3 = (f32[8,8,6]{1,0,2:T(8,128)S(1)}, f32[8,8,6]{1,0,2:T(8,128)}, u32[]{:S(2)}) copy-start(f32[8,8,6]{1,0,2:T(8,128)} %param.8) | copy-start | bytes 4612
  21.8 41.3 %copy-start.1 = (f32[8,8,6,128]{3,1,2,0:T(8,128)S(1)}, f32[8,8,6,128]{3,1,2,0:T(8,128)}, u32[]{:S(2)}) copy-start(f32[8,8,6,128]{3,1,2,0:T(8,128)} %param.5) | copy-start | bytes 589828
  21.8 41.3 %copy-start.2 = (f32[8,8,6,128]{3,1,2,0:T(8,128)S(1)}, f32[8,8,6,128]{3,1,2,0:T(8,128)}, u32[]{:S(2)}) copy-start(f32[8,8,6,128]{3,1,2,0:T(8,128)} %param.6) | copy-start | bytes 589828
  21.8 41.3 %copy-start.4 = (f32[128]{0:T(128)S(1)}, f32[128]{0:T(128)}, u32[]{:S(2)}) copy-start(f32[128]{0:T(128)} %param.9) | copy-start | bytes 1540
  21.8 4.6 %collective-permute-start.3 = (f32[20,6,6,128]{3,1,2,0:T(8,128)S(1)}, f32[20,6,6,128]{3,1,2,0:T(8,128)S(1)}, u32[]{:S(2)}, u32[]{:S(2)}) collective-permute-start(f32[20,6,6,128]{3,1,2,0:T(8,128)S(1)} %get-tuple-element.7), channel_id=1, source_target_pairs={{0,2},{2,4},{4,6},{1,3},{3,5},{5,7},{8,10},{10,12},{12,14},{9,11},... | collective-permute-start | bytes 1105928 | tf_op jit(solution)/shard_map/ppermute | solution.py:24
  26.7 31.7 %collective-permute-start.5 = (f32[20,20,6,128]{3,1,2,0:T(8,128)S(1)}, f32[20,20,6,128]{3,1,2,0:T(8,128)S(1)}, u32[]{:S(2)}, u32[]{:S(2)}) collective-permute-start(f32[20,20,6,128]{3,1,2,0:T(8,128)S(1)} %pad_maximum_fusion), channel_id=1, source_target_pairs={{0,1},{2,3},{4,5},{6,7},{8,9},{10,11},{12,13},{14,15},{16,17},{18,... | collective-permute-start | bytes 3686408 | tf_op jit(solution)/shard_map/ppermute | solution.py:24
  30.2 32.9 %collective-permute-start.4 = (f32[20,20,6,128]{3,1,2,0:T(8,128)S(1)}, f32[20,20,6,128]{3,1,2,0:T(8,128)S(1)}, u32[]{:S(2)}, u32[]{:S(2)}) collective-permute-start(f32[20,20,6,128]{3,1,2,0:T(8,128)S(1)} %pad_maximum_fusion), channel_id=1, source_target_pairs={{1,0},{3,2},{5,4},{7,6},{9,8},{11,10},{13,12},{15,14},{17,16},{19,... | collective-permute-start | bytes 3686408 | tf_op jit(solution)/shard_map/ppermute | solution.py:27
  63.1 1.9 %copy-start = (f32[8,8,6,2048]{3,1,2,0:T(8,128)S(1)}, f32[8,8,6,2048]{3,1,2,0:T(8,128)}, u32[]{:S(2)}) copy-start(f32[8,8,6,2048]{3,1,2,0:T(8,128)} %param.7) | copy-start | bytes 9437188
  68.1 75.7 %all-reduce.2.cloned.1.call-start = ((), (), s32[]{:S(2)}) async-start(), calls=%async_computation.2 | async-start | bytes 262144 | tf_op jit(solution)/shard_map/psum | solution.py:109
  106.8 62.1 %all-gather.2.cloned.1.call-start = ((), (), s32[]{:S(2)}) async-start(), calls=%async_computation.3 | async-start | bytes 1179648 | tf_op jit(solution)/shard_map/all_gather | solution.py:112
Sparse Core Ops, SparseCore 0:
  68.2 38.5 reduce-scatter.1
  109.1 34.6 all-reduce.1
  145.7 23.1 all-gather.1
where the time goes:
time: 183 us
  waiting for transfers between devices  128 us (70%)
  local copies, waits for them, and re-layouts  15.9 us (9%)
  starting transfers between devices  15.7 us (9%)
  between operations  13.9 us (8%)
  matrix products  7.81 us (4%)
    reduce_scatter x1, waiting for transfers between devices, shards(): lax.psum_scatter(partial_intersection, ('gy', 'gz'), scatter_dimension=0,...  38.7 us
    psum x1, waiting for transfers between devices, shards(): share = lax.psum(share, 'gx')  36.9 us
    ppermute x3, waiting for transfers between devices, with_halo(): lax.ppermute(lax.slice_in_dim(block, block.shape[dim] - width, None, axis...  30 us
    all_gather x1, waiting for transfers between devices, shards(): lax.all_gather(share, ('gy', 'gz'), axis=0, tiled=True)  14.8 us
    ppermute x3, starting transfers between devices, with_halo(): lax.ppermute(lax.slice_in_dim(block, block.shape[dim] - width, None, axis...  11.7 us
    ppermute x3, waiting for transfers between devices, with_halo(): lax.ppermute(lax.slice_in_dim(block, 0, width, axis=dim), axis, backward)  7.89 us
    unnamed x16, local copies, waits for them, and re-layouts  7.19 us
    dot_general x1, matrix products, shards(): jnp.dot(flat_occ, lax.all_gather(share, ('gy', 'gz'), axis=0, tiled=True)...  4.81 us
  transfers between devices with their start and end apart: 9, of which 8 were waited for; matrix products, arithmetic and copies ran while one was open for 6% of the time, Pallas kernels for 0%

commit v1 on v0

--- a/solution.py
+++ b/solution.py
@@ -14,6 +14,24 @@
 )
 damping = 0.1
 margin = 6
+
+
+def ring_gather(shard, axis, dim):
+    ways, here, lap = (lax.axis_size(axis), lax.axis_index(axis), shard.shape[dim])
+    shape = [n * ways if d == dim else n for d, n in enumerate(shard.shape)]
+    full = lax.dynamic_update_slice_in_dim(
+        jnp.zeros(shape, shard.dtype), shard, here * lap, axis=dim
+    )
+    going_up = going_down = shard
+    for far in range(1, ways // 2 + 1):
+        going_up = lax.ppermute(going_up, axis, [(d, (d + 1) % ways) for d in range(ways)])
+        full = lax.dynamic_update_slice_in_dim(full, going_up, (here - far) % ways * lap, axis=dim)
+        if 2 * far < ways:
+            going_down = lax.ppermute(going_down, axis, [(d, (d - 1) % ways) for d in range(ways)])
+            full = lax.dynamic_update_slice_in_dim(
+                full, going_down, (here + far) % ways * lap, axis=dim
+            )
+    return full
 
 
 def with_halo(block, sides, width):
@@ -109,7 +127,7 @@
     share = lax.psum(share, "gx")
     removed = jnp.dot(
         flat_occ,
-        lax.all_gather(share, ("gy", "gz"), axis=0, tiled=True),
+        ring_gather(share, ("gy", "gz"), 0),
         precision=lax.Precision.HIGHEST,
         preferred_element_type=jnp.float32,
     )

time: 183 us -> 190 us (1.038)
  starting transfers between devices: 15.7 us -> 24.6 us
  waiting for transfers between devices: 128 us -> 124 us
  local copies, waits for them, and re-layouts: 15.9 us -> 19 us
    all_gather x1 -> x0, waiting for transfers between devices: 14.8 us -> none  [shards(): lax.all_gather(share, ('gy', 'gz'), axis=0, tiled=True)]
    ppermute x0 -> x7, waiting for transfers between devices: none -> 10.1 us  [the longest x4 7.46 us: ring_gather(): lax.ppermute(going_up, axis, [(d, (d + 1) % ways) for d in range(ways)])]
    ppermute x0 -> x7, starting transfers between devices: none -> 8.97 us  [the longest x4 8.28 us: ring_gather(): lax.ppermute(going_up, axis, [(d, (d + 1) % ways) for d in range(ways)])]
    dynamic_update_slice x0 -> x8, local copies, waits for them, and re-layouts: none -> 2.86 us  [the longest x4 0.98 us: ring_gather(): lax.dynamic_update_slice_in_dim(full, going_up, (here - far) % ways * lap...]
  transfers between devices with their start and end apart: 9 -> 15, of which waited for: 8 -> 11; matrix products, arithmetic and copies ran while one was open for 6% -> 8% of each run, Pallas kernels for 0% -> 0%
where the time goes in v1:
time: 190 us; the launch traced here: 189 us
  waiting for transfers between devices  124 us (65%)
  starting transfers between devices  24.6 us (13%)
  local copies, waits for them, and re-layouts  19 us (10%)
  between operations  14.3 us (8%)
  matrix products  6.62 us (3%)
    reduce_scatter x1, waiting for transfers between devices, shards(): lax.psum_scatter(partial_intersection, ('gy', 'gz'), scatter_dimension=0,...  38.7 us
    psum x1, waiting for transfers between devices, shards(): share = lax.psum(share, 'gx')  37 us
    ppermute x3, waiting for transfers between devices, with_halo(): lax.ppermute(lax.slice_in_dim(block, block.shape[dim] - width, None, axis...  30 us
    ppermute x3, starting transfers between devices, with_halo(): lax.ppermute(lax.slice_in_dim(block, block.shape[dim] - width, None, axis...  11.7 us
    ppermute x4, starting transfers between devices, ring_gather(): lax.ppermute(going_up, axis, [(d, (d + 1) % ways) for d in range(ways)])  8.28 us
    ppermute x3, waiting for transfers between devices, with_halo(): lax.ppermute(lax.slice_in_dim(block, 0, width, axis=dim), axis, backward)  7.89 us
    ppermute x4, waiting for transfers between devices, ring_gather(): lax.ppermute(going_up, axis, [(d, (d + 1) % ways) for d in range(ways)])  7.46 us
    unnamed x16, local copies, waits for them, and re-layouts  7.34 us
  transfers between devices with their start and end apart: 15, of which 11 were waited for; matrix products, arithmetic and copies ran while one was open for 8% of the time, Pallas kernels for 0%

profile of v1, /device:TPU:0, one launch (start us, length us, event | category | flops | bytes accessed | tf_op | source)
XLA Modules:
  0.0 189.5 jit_solution(12587301395120240177)
XLA Ops:
  7.2 0.0 reduce-scatter.2.cloned.1.call-start
  7.2 1.0 fusion.49
  8.2 5.0 %collective-permute-start.1 = (f32[6,8,6,128]{3,1,2,0:T(8,128)S(1)}, f32[6,8,6,128]{3,1,2,0:T(8,128)S(1)}, u32[]{:S(2)}, u32[]{:S(2)}) collective-permute-start(f32[6,8,6,128]{3,1,2,0:T(8,128)S(1)} %get-tuple-element.12), channel_id=1, source_target_pairs={{0,8},{8,16},{16,24},{1,9},{9,17},{17,25},{2,10},{10,18},{18,26},{... | collective-permute-start | bytes 442376 | tf_op jit(solution)/shard_map/ppermute | solution.py:42
  13.2 1.3 collective-permute-start
  14.5 1.8 collective-permute-done.1
  16.3 1.0 constant_dynamic-update-slice_fusion.1
  17.3 3.1 %collective-permute-done = f32[6,8,6,128]{3,1,2,0:T(8,128)S(1)} collective-permute-done((f32[6,8,6,128]{3,1,2,0:T(8,128)S(1)}, f32[6,8,6,128]{3,1,2,0:T(8,128)S(1)}, u32[]{:S(2)}, u32[]{:S(2)}) %collective-permute-start) | collective-permute-done | bytes 147488 | tf_op jit(solution)/shard_map/ppermute | solution.py:45
  20.4 0.1 fusion.48
  20.5 1.3 collective-permute-start.2
  21.8 0.0 copy-start.1
  21.8 3.2 %collective-permute-start.3 = (f32[20,6,6,128]{3,1,2,0:T(8,128)S(1)}, f32[20,6,6,128]{3,1,2,0:T(8,128)S(1)}, u32[]{:S(2)}, u32[]{:S(2)}) collective-permute-start(f32[20,6,6,128]{3,1,2,0:T(8,128)S(1)} %get-tuple-element.7), channel_id=1, source_target_pairs={{0,2},{2,4},{4,6},{1,3},{3,5},{5,7},{8,10},{10,12},{12,14},{9,11},... | collective-permute-start | bytes 1105928 | tf_op jit(solution)/shard_map/ppermute | solution.py:42
  25.1 1.4 collective-permute-done.3
  26.5 0.2 pad_maximum_fusion
  26.7 3.5 %collective-permute-start.5 = (f32[20,20,6,128]{3,1,2,0:T(8,128)S(1)}, f32[20,20,6,128]{3,1,2,0:T(8,128)S(1)}, u32[]{:S(2)}, u32[]{:S(2)}) collective-permute-start(f32[20,20,6,128]{3,1,2,0:T(8,128)S(1)} %pad_maximum_fusion), channel_id=1, source_target_pairs={{0,1},{2,3},{4,5},{6,7},{8,9},{10,11},{12,13},{14,15},{16,17},{18,... | collective-permute-start | bytes 3686408 | tf_op jit(solution)/shard_map/ppermute | solution.py:42
  30.2 1.3 collective-permute-start.4
  31.6 26.8 %collective-permute-done.5 = f32[20,20,6,128]{3,1,2,0:T(8,128)S(1)} collective-permute-done((f32[20,20,6,128]{3,1,2,0:T(8,128)S(1)}, f32[20,20,6,128]{3,1,2,0:T(8,128)S(1)}, u32[]{:S(2)}, u32[]{:S(2)}) %collective-permute-start.5) | collective-permute-done | bytes 1228832 | tf_op jit(solution)/shard_map/ppermute | solution.py:42
  58.4 4.8 %collective-permute-done.4 = f32[20,20,6,128]{3,1,2,0:T(8,128)S(1)} collective-permute-done((f32[20,20,6,128]{3,1,2,0:T(8,128)S(1)}, f32[20,20,6,128]{3,1,2,0:T(8,128)S(1)}, u32[]{:S(2)}, u32[]{:S(2)}) %collective-permute-start.4) | collective-permute-done | bytes 1228832 | tf_op jit(solution)/shard_map/ppermute | solution.py:45
  63.2 0.9 fusion.10
  64.1 1.0 copy-done
  65.0 3.0 %convolution_bitcast_fusion = f32[2048,128]{0,1:T(8,128)} fusion(f32[8,8,6,128]{3,1,2,0:T(8,128)S(1)} %fusion.10, f32[8,8,6,2048]{3,1,2,0:T(8,128)S(1)} %copy-done), kind=kOutput, calls=%fused_computation | convolution fusion | flops 1207959552 | bytes 4390912 | tf_op jit(solution)/shard_map/dot_general | solution.py:119
  68.1 0.0 reduce-scatter.2.cloned.1.call-update
  68.1 0.0 all-reduce.2.cloned.1.call-start
  68.1 38.7 %reduce-scatter.2.cloned.1.call-done = f32[256,128]{0,1:T(8,128)} async-done(((f32[2048,128]{0,1:T(8,128)}), f32[256,128]{0,1:T(8,128)}) %reduce-scatter.2.cloned.1.call-update) | async-done | bytes 131088 | tf_op jit(solution)/shard_map/reduce_scatter | solution.py:126
  106.8 0.0 all-reduce.2.cloned.1.call-update
  106.8 37.0 %all-reduce.2.cloned.1.call-done = f32[256,128]{0,1:T(8,128)} async-done(((f32[256,128]{0,1:T(8,128)}), f32[256,128]{0,1:T(8,128)}) %all-reduce.2.cloned.1.call-update) | async-done | bytes 131088 | tf_op jit(solution)/shard_map/psum | solution.py:127
  143.8 2.0 %collective-permute-start.6 = (f32[256,128]{0,1:T(8,128)}, f32[256,128]{0,1:T(8,128)}, u32[]{:S(2)}, u32[]{:S(2)}) collective-permute-start(f32[256,128]{0,1:T(8,128)} %all-reduce.2.cloned.1.call-done), channel_id=1, source_target_pairs={{0,1},{1,2},{2,3},{3,4},{4,5},{5,6},{6,7},{7,0},{8,9},{9,10},{10,1... | collective-permute-start | bytes 393224 | tf_op jit(solution)/shard_map/ppermute | solution.py:27
  145.8 3.9 %copy.13 = f32[8,8,6,2048]{3,2,1,0:T(8,128)} copy(f32[8,8,6,2048]{3,1,2,0:T(8,128)S(1)} %copy-done) | data formatting | bytes 6291456 | tf_op args[2]
  149.8 3.1 %reshape.16 = f32[384,2048]{1,0:T(8,128)S(1)} reshape(f32[8,8,6,2048]{3,2,1,0:T(8,128)} %copy.13) | data formatting | bytes 6291456 | tf_op jit(solution)/shard_map/reshape | solution.py:114
  152.9 0.7 copy.12
  153.6 1.6 reshape.15
  155.3 1.1 copy.14
  156.3 0.1 broadcast_in_dim.2
  156.4 0.9 constant_dynamic-update-slice_fusion.14
  157.4 0.7 collective-permute-start.9
  158.1 1.4 collective-permute-start.8
  159.5 0.9 constant_dynamic-update-slice_fusion.13
  160.4 0.9 constant_dynamic-update-slice_fusion.12
  161.3 2.7 %collective-permute-done.9 = f32[256,128]{0,1:T(8,128)S(1)} collective-permute-done((f32[256,128]{0,1:T(8,128)}, f32[256,128]{0,1:T(8,128)S(1)}, u32[]{:S(2)}, u32[]{:S(2)}) %collective-permute-start.9) | collective-permute-done | bytes 131104 | tf_op jit(solution)/shard_map/ppermute | solution.py:30
  164.0 0.6 collective-permute-done.8
  164.6 2.4 %collective-permute-start.10 = (f32[256,128]{0,1:T(8,128)S(1)}, f32[256,128]{0,1:T(8,128)S(1)}, u32[]{:S(2)}, u32[]{:S(2)}) collective-permute-start(f32[256,128]{0,1:T(8,128)S(1)} %collective-permute-done.8), channel_id=1, source_target_pairs={{0,1},{1,2},{2,3},{3,4},{4,5},{5,6},{6,7},{7,0},{8,9},{9,10},{10,1... | collective-permute-start | bytes 393224 | tf_op jit(solution)/shard_map/ppermute | solution.py:27
  167.1 3.8 %collective-permute-done.10 = f32[256,128]{0,1:T(8,128)S(1)} collective-permute-done((f32[256,128]{0,1:T(8,128)S(1)}, f32[256,128]{0,1:T(8,128)S(1)}, u32[]{:S(2)}, u32[]{:S(2)}) %collective-permute-start.10) | collective-permute-done | bytes 131104 | tf_op jit(solution)/shard_map/ppermute | solution.py:27
  170.9 2.5 %collective-permute-start.12 = (f32[256,128]{0,1:T(8,128)S(1)}, f32[256,128]{0,1:T(8,128)S(1)}, u32[]{:S(2)}, u32[]{:S(2)}) collective-permute-start(f32[256,128]{0,1:T(8,128)S(1)} %collective-permute-done.10), channel_id=1, source_target_pairs={{0,1},{1,2},{2,3},{3,4},{4,5},{5,6},{6,7},{7,0},{8,9},{9,10},{10,1... | collective-permute-start | bytes 393224 | tf_op jit(solution)/shard_map/ppermute | solution.py:27
  173.4 3.0 %collective-permute-done.12 = f32[256,128]{0,1:T(8,128)S(1)} collective-permute-done((f32[256,128]{0,1:T(8,128)S(1)}, f32[256,128]{0,1:T(8,128)S(1)}, u32[]{:S(2)}, u32[]{:S(2)}) %collective-permute-start.12) | collective-permute-done | bytes 131104 | tf_op jit(solution)/shard_map/ppermute | solution.py:27
  176.4 3.6 %fusion = f32[384,128]{0,1:T(8,128)} fusion(f32[384,128]{0,1:T(8,128)S(1)} %copy.14, f32[2048,128]{0,1:T(8,128)S(1)} %constant_dynamic-update-slice_fusion.7, f32[384,2048]{1,0:T(8,128)S(1)} %reshape.16), kind=kOutput, calls=%fused_computation.23 | convolution fusion | flops 1208008704 | bytes 4587520 | tf_op jit(solution)/shard_map/dot_general | solution.py:128
  180.0 1.1 copy.15
  181.1 0.7 copy.18
  181.8 0.1 copy_subtract_fusion
  181.9 0.7 copy.17
  (23 shorter events, 0.2 us)
Async XLA Ops:
  7.2 99.6 %reduce-scatter.2.cloned.1.call-start = ((), (), s32[]{:S(2)}) async-start(), calls=%async_computation.1 | async-start | bytes 1179648 | tf_op jit(solution)/shard_map/reduce_scatter | solution.py:126
  8.2 8.1 %collective-permute-start.1 = (f32[6,8,6,128]{3,1,2,0:T(8,128)S(1)}, f32[6,8,6,128]{3,1,2,0:T(8,128)S(1)}, u32[]{:S(2)}, u32[]{:S(2)}) collective-permute-start(f32[6,8,6,128]{3,1,2,0:T(8,128)S(1)} %get-tuple-element.12), channel_id=1, source_target_pairs={{0,8},{8,16},{16,24},{1,9},{9,17},{17,25},{2,10},{10,18},{18,26},{... | collective-permute-start | bytes 442376 | tf_op jit(solution)/shard_map/ppermute | solution.py:42
  13.2 7.2 %collective-permute-start = (f32[6,8,6,128]{3,1,2,0:T(8,128)S(1)}, f32[6,8,6,128]{3,1,2,0:T(8,128)S(1)}, u32[]{:S(2)}, u32[]{:S(2)}) collective-permute-start(f32[6,8,6,128]{3,1,2,0:T(8,128)S(1)} %get-tuple-element.11), channel_id=1, source_target_pairs={{8,0},{16,8},{24,16},{9,1},{17,9},{25,17},{10,2},{18,10},{26,18},{... | collective-permute-start | bytes 442376 | tf_op jit(solution)/shard_map/ppermute | solution.py:45
  20.5 4.6 %collective-permute-start.2 = (f32[20,6,6,128]{3,1,2,0:T(8,128)S(1)}, f32[20,6,6,128]{3,1,2,0:T(8,128)S(1)}, u32[]{:S(2)}, u32[]{:S(2)}) collective-permute-start(f32[20,6,6,128]{3,1,2,0:T(8,128)S(1)} %get-tuple-element.6), channel_id=1, source_target_pairs={{2,0},{4,2},{6,4},{3,1},{5,3},{7,5},{10,8},{12,10},{14,12},{11,9},... | collective-permute-start | bytes 1105928 | tf_op jit(solution)/shard_map/ppermute | solution.py:45
  21.8 9.7 %copy-start.3 = (f32[8,8,6]{1,0,2:T(8,128)S(1)}, f32[8,8,6]{1,0,2:T(8,128)}, u32[]{:S(2)}) copy-start(f32[8,8,6]{1,0,2:T(8,128)} %param.8) | copy-start | bytes 4612
  21.8 41.3 %copy-start.1 = (f32[8,8,6,128]{3,1,2,0:T(8,128)S(1)}, f32[8,8,6,128]{3,1,2,0:T(8,128)}, u32[]{:S(2)}) copy-start(f32[8,8,6,128]{3,1,2,0:T(8,128)} %param.5) | copy-start | bytes 589828
  21.8 41.3 %copy-start.2 = (f32[8,8,6,128]{3,1,2,0:T(8,128)S(1)}, f32[8,8,6,128]{3,1,2,0:T(8,128)}, u32[]{:S(2)}) copy-start(f32[8,8,6,128]{3,1,2,0:T(8,128)} %param.6) | copy-start | bytes 589828
  21.8 41.3 %copy-start.4 = (f32[128]{0:T(128)S(1)}, f32[128]{0:T(128)}, u32[]{:S(2)}) copy-start(f32[128]{0:T(128)} %param.9) | copy-start | bytes 1540
  21.8 4.6 %collective-permute-start.3 = (f32[20,6,6,128]{3,1,2,0:T(8,128)S(1)}, f32[20,6,6,128]{3,1,2,0:T(8,128)S(1)}, u32[]{:S(2)}, u32[]{:S(2)}) collective-permute-start(f32[20,6,6,128]{3,1,2,0:T(8,128)S(1)} %get-tuple-element.7), channel_id=1, source_target_pairs={{0,2},{2,4},{4,6},{1,3},{3,5},{5,7},{8,10},{10,12},{12,14},{9,11},... | collective-permute-start | bytes 1105928 | tf_op jit(solution)/shard_map/ppermute | solution.py:42
  26.7 31.7 %collective-permute-start.5 = (f32[20,20,6,128]{3,1,2,0:T(8,128)S(1)}, f32[20,20,6,128]{3,1,2,0:T(8,128)S(1)}, u32[]{:S(2)}, u32[]{:S(2)}) collective-permute-start(f32[20,20,6,128]{3,1,2,0:T(8,128)S(1)} %pad_maximum_fusion), channel_id=1, source_target_pairs={{0,1},{2,3},{4,5},{6,7},{8,9},{10,11},{12,13},{14,15},{16,17},{18,... | collective-permute-start | bytes 3686408 | tf_op jit(solution)/shard_map/ppermute | solution.py:42
  30.2 32.9 %collective-permute-start.4 = (f32[20,20,6,128]{3,1,2,0:T(8,128)S(1)}, f32[20,20,6,128]{3,1,2,0:T(8,128)S(1)}, u32[]{:S(2)}, u32[]{:S(2)}) collective-permute-start(f32[20,20,6,128]{3,1,2,0:T(8,128)S(1)} %pad_maximum_fusion), channel_id=1, source_target_pairs={{1,0},{3,2},{5,4},{7,6},{9,8},{11,10},{13,12},{15,14},{17,16},{19,... | collective-permute-start | bytes 3686408 | tf_op jit(solution)/shard_map/ppermute | solution.py:45
  63.1 1.9 copy-start
  68.1 75.7 %all-reduce.2.cloned.1.call-start = ((), (), s32[]{:S(2)}) async-start(), calls=%async_computation.2 | async-start | bytes 262144 | tf_op jit(solution)/shard_map/psum | solution.py:127
  143.8 13.6 %collective-permute-start.7 = (f32[256,128]{0,1:T(8,128)}, f32[256,128]{0,1:T(8,128)}, u32[]{:S(2)}, u32[]{:S(2)}) collective-permute-start(f32[256,128]{0,1:T(8,128)} %all-reduce.2.cloned.1.call-done), channel_id=1, source_target_pairs={{0,7},{1,0},{2,1},{3,2},{4,3},{5,4},{6,5},{7,6},{8,15},{9,8},{10,9... | collective-permute-start | bytes 393224 | tf_op jit(solution)/shard_map/ppermute | solution.py:30
  143.8 14.2 %collective-permute-start.6 = (f32[256,128]{0,1:T(8,128)}, f32[256,128]{0,1:T(8,128)}, u32[]{:S(2)}, u32[]{:S(2)}) collective-permute-start(f32[256,128]{0,1:T(8,128)} %all-reduce.2.cloned.1.call-done), channel_id=1, source_target_pairs={{0,1},{1,2},{2,3},{3,4},{4,5},{5,6},{6,7},{7,0},{8,9},{9,10},{10,1... | collective-permute-start | bytes 393224 | tf_op jit(solution)/shard_map/ppermute | solution.py:27
  157.4 6.6 %collective-permute-start.9 = (f32[256,128]{0,1:T(8,128)}, f32[256,128]{0,1:T(8,128)S(1)}, u32[]{:S(2)}, u32[]{:S(2)}) collective-permute-start(f32[256,128]{0,1:T(8,128)} %collective-permute-done.7), channel_id=1, source_target_pairs={{0,7},{1,0},{2,1},{3,2},{4,3},{5,4},{6,5},{7,6},{8,15},{9,8},{10,9... | collective-permute-start | bytes 393224 | tf_op jit(solution)/shard_map/ppermute | solution.py:30
  158.1 6.6 %collective-permute-start.8 = (f32[256,128]{0,1:T(8,128)}, f32[256,128]{0,1:T(8,128)S(1)}, u32[]{:S(2)}, u32[]{:S(2)}) collective-permute-start(f32[256,128]{0,1:T(8,128)} %collective-permute-done.6), channel_id=1, source_target_pairs={{0,1},{1,2},{2,3},{3,4},{4,5},{5,6},{6,7},{7,0},{8,9},{9,10},{10,1... | collective-permute-start | bytes 393224 | tf_op jit(solution)/shard_map/ppermute | solution.py:27
  164.0 9.4 %collective-permute-start.11 = (f32[256,128]{0,1:T(8,128)S(1)}, f32[256,128]{0,1:T(8,128)S(1)}, u32[]{:S(2)}, u32[]{:S(2)}) collective-permute-start(f32[256,128]{0,1:T(8,128)S(1)} %collective-permute-done.9), channel_id=1, source_target_pairs={{0,7},{1,0},{2,1},{3,2},{4,3},{5,4},{6,5},{7,6},{8,15},{9,8},{10,9... | collective-permute-start | bytes 393224 | tf_op jit(solution)/shard_map/ppermute | solution.py:30
  164.6 6.3 %collective-permute-start.10 = (f32[256,128]{0,1:T(8,128)S(1)}, f32[256,128]{0,1:T(8,128)S(1)}, u32[]{:S(2)}, u32[]{:S(2)}) collective-permute-start(f32[256,128]{0,1:T(8,128)S(1)} %collective-permute-done.8), channel_id=1, source_target_pairs={{0,1},{1,2},{2,3},{3,4},{4,5},{5,6},{6,7},{7,0},{8,9},{9,10},{10,1... | collective-permute-start | bytes 393224 | tf_op jit(solution)/shard_map/ppermute | solution.py:27
  170.9 5.5 %collective-permute-start.12 = (f32[256,128]{0,1:T(8,128)S(1)}, f32[256,128]{0,1:T(8,128)S(1)}, u32[]{:S(2)}, u32[]{:S(2)}) collective-permute-start(f32[256,128]{0,1:T(8,128)S(1)} %collective-permute-done.10), channel_id=1, source_target_pairs={{0,1},{1,2},{2,3},{3,4},{4,5},{5,6},{6,7},{7,0},{8,9},{9,10},{10,1... | collective-permute-start | bytes 393224 | tf_op jit(solution)/shard_map/ppermute | solution.py:27
Sparse Core Ops, SparseCore 0:
  68.2 38.5 reduce-scatter.1
  109.1 34.6 all-reduce.1
